TPU v7x, 32 devices: a whole 2x2x4 slice. The times are simulated.
32 devices in a mesh: state: 8 (over y, x, core), snap: 4 (over z).
Axes of the slice: x: 2, y: 2, z: 4, core: 2. Of those that a mesh axis runs over, the one named last changes fastest.
Arguments:
- obs_factor: bfloat16 [8192, 8, 512], P('state', None, 'snap'), may hold values from -1.8920169 to 1.8920169
- ctrl_factor: bfloat16 [8192, 512], P('state', 'snap'), may hold values from -1.6817928 to 1.6817928
- support: int32 [64, 4], P('state'), may hold values from 0 to 1
Outputs:
- cross: float32 [8, 512, 512], P(None, 'snap', 'state')
All inputs are finite; a program needn't handle non-finite values.
Results may differ from a plain program's by a relative error of at most 0.0006.
Values may be sent and summed in bfloat16 or wider, within the bound.
A program may use at most 64 MiB of HBM per device.

v0:
```python
import functools

import jax
import jax.numpy as jnp
from jax import lax
from jax.experimental import pallas as pl
from jax.experimental.pallas import tpu as pltpu
from jax.sharding import PartitionSpec as P

MESH = pl.DeviceIdType.MESH
CORES = 2
SIDE = 2
PLANE = CORES * SIDE * SIDE
LINE = SIDE * SIDE
QS = 4
RELAY_FROM = QS // 2
BEHIND_MIDDLE = 4
BEHIND_END = 2
PAIR = 2
RELAY_AT = {2: 0, 3: 2, 4: 8, 5: 8, 6: 10, 7: 12}
VMEM_BYTES = 52 * 1024 * 1024


def cross_kernel(
    support,
    obs_hbm,
    ctrl_hbm,
    out,
    obs_raw,
    ctrl_raw,
    wide,
    obs,
    own_t,
    ctrl_t,
    part,
    far,
    near,
    ld_sem,
    obs_send,
    obs_recv,
    own_send,
    pair_send,
    fwd_send,
    ctrl_recv,
    half_send,
    half_recv,
    far_send,
    far_recv,
):
    s = lax.axis_index("state")
    z = lax.axis_index("snap")
    row_blocks = support.shape[1]
    rows, windows, cols = obs_hbm.shape
    block = rows // row_blocks
    piece = ctrl_t.shape[3]
    h = s % CORES
    chip = s // CORES
    ax = chip % SIDE
    ay = chip // SIDE
    pair = chip * CORES + (1 - h)
    x_next = (ay * SIDE + (1 - ax)) * CORES + h
    y_next = ((1 - ay) * SIDE + ax) * CORES + h
    last = LINE - 1
    middle = jnp.logical_and(z > 0, z < last)

    def load_ctrl():
        return pltpu.make_async_copy(ctrl_hbm, ctrl_raw, ld_sem.at[row_blocks])

    def load_obs(k):
        span = pl.ds(k * block, block)
        return pltpu.make_async_copy(obs_hbm.at[span], obs_raw.at[span], ld_sem.at[k])

    load_ctrl().start()
    for k in range(row_blocks):
        load_obs(k).start()

    barrier = pltpu.get_barrier_semaphore()

    def greet(state, snap):
        pl.semaphore_signal(barrier, inc=1, device_id=(state, snap), device_id_type=MESH)

    greet(pair, z)
    greet(x_next, z)
    greet(y_next, z)

    @pl.when(z > 0)
    def _():
        greet(s, z - 1)
        greet(pair, z - 1)

    @pl.when(z < last)
    def _():
        greet(s, z + 1)
        greet(pair, z + 1)

    load_ctrl().wait()
    for k in range(row_blocks):
        span = slice(k * block, (k + 1) * block)
        keep = support[z, k].astype(jnp.float32)
        kept = ctrl_raw[span, :] * keep.astype(jnp.bfloat16)
        turned = kept.T
        own_t[:, :, span] = turned.reshape(CORES * QS, piece, block)

    @pl.when(middle)
    def _():
        pl.semaphore_wait(barrier, 7)

    @pl.when(jnp.logical_not(middle))
    def _():
        pl.semaphore_wait(barrier, 5)

    def own_copy(side, q, g):
        state = chip * CORES + g
        snap = z + 2 * side - 1
        return pltpu.make_async_remote_copy(
            src_ref=own_t.at[g * QS + q],
            dst_ref=ctrl_t.at[z, q, h],
            send_sem=own_send.at[side, q, g],
            recv_sem=ctrl_recv.at[z, q, h],
            device_id=(state, snap),
            device_id_type=MESH,
        )

    def pair_copy(q):
        return pltpu.make_async_remote_copy(
            src_ref=own_t.at[(1 - h) * QS + q],
            dst_ref=ctrl_t.at[z, q, h],
            send_sem=pair_send.at[q],
            recv_sem=ctrl_recv.at[z, q, h],
            device_id=(pair, z),
            device_id_type=MESH,
        )

    def fwd_copy(b, q, hs, snap):
        return pltpu.make_async_remote_copy(
            src_ref=ctrl_t.at[b, q, hs],
            dst_ref=ctrl_t.at[b, q, hs],
            send_sem=fwd_send.at[b, q, hs],
            recv_sem=ctrl_recv.at[b, q, hs],
            device_id=(s, snap),
            device_id_type=MESH,
        )

    def arrived(b, q, hs):
        fwd_copy(b, q, hs, z).wait_recv()

    for q in range(QS):
        for g in range(CORES):

            @pl.when(z > 0)
            def _():
                own_copy(0, q, g).start()

            @pl.when(z < last)
            def _():
                own_copy(1, q, g).start()

    for q in range(QS):
        pair_copy(q).start()
        ctrl_t[z, q, h] = own_t[h * QS + q]

    def obs_copy(k):
        span = pl.ds(pl.multiple_of(k * block, block), block)
        return pltpu.make_async_remote_copy(
            src_ref=obs.at[h, span],
            dst_ref=obs.at[h, span],
            send_sem=obs_send.at[k],
            recv_sem=obs_recv.at[k],
            device_id=(pair, z),
            device_id_type=MESH,
        )

    def arrange(k, _):
        load_obs(k).wait()
        span = pl.ds(pl.multiple_of(k * block, block), block)
        keep = support[z, k].astype(jnp.float32)
        raw = obs_raw[span].astype(jnp.float32) * keep
        wide[...] = raw.reshape(block * windows, cols)
        for w in range(windows):
            obs[h, span, w * cols : (w + 1) * cols] = wide[
                pl.ds(w, block, stride=windows), :
            ].astype(jnp.bfloat16)
        obs_copy(k).start()
        return 0

    lax.fori_loop(0, row_blocks, arrange, 0)

    def pass_on(d, q):
        @pl.when(jnp.logical_and(middle, z - d >= 0))
        def _():
            for hs in range(CORES):
                arrived(z - d, q, hs)
                fwd_copy(z - d, q, hs, z + 1).start()

        @pl.when(jnp.logical_and(middle, z + d <= last))
        def _():
            for hs in range(CORES):
                arrived(z + d, q, hs)
                fwd_copy(z + d, q, hs, z - 1).start()

    def block_at(k):
        up = jnp.where(k == 0, 0, jnp.where(k == 1, 1, jnp.where(k == 2, 2, 3)))
        one = jnp.where(k == 0, 1, jnp.where(k == 1, 2, jnp.where(k == 2, 0, 3)))
        return jnp.where(
            z == 0, up, jnp.where(z == last, last - up, jnp.where(z == 1, one, last - one))
        )

    def half_copy(kind, q, rows_half, b, state):
        return pltpu.make_async_remote_copy(
            src_ref=part.at[b, q, rows_half],
            dst_ref=far.at[kind, q],
            send_sem=half_send.at[kind, q],
            recv_sem=half_recv.at[kind, q],
            device_id=(state, z),
            device_id_type=MESH,
        )

    def near_copy(kind, q, rows_half, b, state):
        return pltpu.make_async_remote_copy(
            src_ref=part.at[b, q, rows_half],
            dst_ref=near.at[kind, q, rows_half],
            send_sem=far_send.at[kind, q, rows_half],
            recv_sem=far_recv.at[kind, q, rows_half],
            device_id=(state, z),
            device_id_type=MESH,
        )

    def role(b):
        same_x = b % SIDE == ax
        same_y = b // SIDE == ay
        kind = jnp.where(same_x, 1, 0)
        beside = same_x != same_y
        corner = jnp.logical_and(jnp.logical_not(same_x), jnp.logical_not(same_y))
        return kind, beside, corner

    def finished(t):
        behind = jnp.where(middle, BEHIND_MIDDLE, BEHIND_END)
        return jnp.maximum(jnp.minimum(2 * t - 3 * QS, t - behind), 0)

    def finish(t, _):
        b = block_at(t // QS)
        q = t % QS
        kind, beside, _ = role(b)

        @pl.when(beside)
        def _():
            half_copy(kind, q, kind, b, y_next).wait_recv()
            part[b, q, kind] = part[b, q, kind] + far[kind, q]
            near_copy(kind, q, kind, b, jnp.where(kind == 1, y_next, x_next)).start()

        return 0

    tile = 2 * cols
    width = obs.shape[2]

    def turn(t, before, count):
        b = block_at(t // QS)
        q = t % QS

        for k, when in RELAY_AT.items():

            @pl.when(t == when)
            def _():
                pass_on(1 + k // QS, k % QS)

        @pl.when(t < QS)
        def _():
            for i in range(count):
                arrived(b, q + i, 1 - h)

        @pl.when(jnp.logical_and(t >= QS, jnp.logical_not(middle)))
        def _():
            for i in range(count):
                for hs in range(CORES):
                    arrived(b, q + i, hs)

        left = [
            ctrl_t[b, pl.ds(q, count), hs].reshape(count * piece, obs.shape[1])
            for hs in range(CORES)
        ]
        for n in range(0, width, tile):
            total = sum(
                jnp.dot(
                    left[hs], obs[hs, :, n : n + tile], preferred_element_type=jnp.float32
                )
                for hs in range(CORES)
            )
            part[b, pl.ds(q, count), :, :, n : n + tile] = total.reshape(
                count, 2, piece // 2, tile
            )

        kind, beside, corner = role(b)

        @pl.when(beside)
        def _():
            for i in range(count):
                state = jnp.where(kind == 1, y_next, x_next)
                near_copy(kind, q + i, 1 - kind, b, state).start()

        @pl.when(corner)
        def _():
            for i in range(count):
                half_copy(0, q + i, 0, b, y_next).start()
                half_copy(1, q + i, 1, b, x_next).start()

        lax.fori_loop(before, finished(t), finish, 0)
        return 0

    paired = (LINE - 1) * QS

    def double(i, _):
        t = i * PAIR
        return turn(t, finished(t - PAIR), PAIR)

    def single(i, _):
        t = paired + i
        return turn(t, finished(jnp.where(i == 0, t - PAIR, t - 1)), 1)

    for k in range(RELAY_FROM):
        pass_on(1, k)
    for k in range(row_blocks):
        obs_copy(k).wait_recv()
    lax.fori_loop(0, paired // PAIR, double, 0)
    lax.fori_loop(0, QS, single, 0)
    lax.fori_loop(finished(LINE * QS - 1), LINE * QS, finish, 0)

    for q in range(QS):
        for r in range(2):
            for kind in range(2):
                near_copy(kind, q, r, chip, s).wait_recv()
            total = part[chip, q, r] + near[0, q, r] + near[1, q, r]
            base = (q * 2 + r) * (piece // 2)
            for w in range(windows):
                out[w, base : base + piece // 2, :] = total[:, w * cols : (w + 1) * cols]

    for q in range(QS):
        for kind in range(2):
            half_copy(kind, q, kind, chip, y_next).wait_send()
            for r in range(2):
                near_copy(kind, q, r, chip, y_next).wait_send()
        pair_copy(q).wait_send()
        for g in range(CORES):

            @pl.when(z > 0)
            def _():
                own_copy(0, q, g).wait_send()

            @pl.when(z < last)
            def _():
                own_copy(1, q, g).wait_send()

        for d in range(1, LINE - 1):
            for hs in range(CORES):

                @pl.when(jnp.logical_and(middle, z - d >= 0))
                def _():
                    fwd_copy(z - d, q, hs, z).wait_send()

                @pl.when(jnp.logical_and(middle, z + d <= last))
                def _():
                    fwd_copy(z + d, q, hs, z).wait_send()

    for k in range(row_blocks):
        obs_copy(k).wait_send()


def plane_local(obs_factor, ctrl_factor, support):
    rows, windows, cols = obs_factor.shape
    row_blocks = support.shape[0]
    piece = cols // (CORES * QS)
    width = windows * cols
    bf16, f32 = jnp.bfloat16, jnp.float32
    dma = pltpu.SemaphoreType.DMA
    turned = pl.pallas_call(
        cross_kernel,
        out_shape=jax.ShapeDtypeStruct((windows, cols // CORES, cols), f32),
        in_specs=[
            pl.BlockSpec(memory_space=pltpu.SMEM),
            pl.BlockSpec(memory_space=pltpu.HBM),
            pl.BlockSpec(memory_space=pltpu.HBM),
        ],
        out_specs=pl.BlockSpec(memory_space=pltpu.VMEM),
        scratch_shapes=[
            pltpu.VMEM((rows, windows, cols), bf16),
            pltpu.VMEM((rows, cols), bf16),
            pltpu.VMEM((rows // row_blocks * windows, cols), f32),
            pltpu.VMEM((CORES, rows, width), bf16),
            pltpu.VMEM((CORES * QS, piece, rows), bf16),
            pltpu.VMEM((LINE, QS, CORES, piece, rows), bf16),
            pltpu.VMEM((LINE, QS, 2, piece // 2, width), f32),
            pltpu.VMEM((2, QS, piece // 2, width), f32),
            pltpu.VMEM((2, QS, 2, piece // 2, width), f32),
            dma((row_blocks + 1,)),
            dma((row_blocks,)),
            dma((row_blocks,)),
            dma((2, QS, CORES)),
            dma((QS,)),
            dma((LINE, QS, CORES)),
            dma((LINE, QS, CORES)),
            dma((2, QS)),
            dma((2, QS)),
            dma((2, QS, 2)),
            dma((2, QS, 2)),
        ],
        compiler_params=pltpu.CompilerParams(
            collective_id=0, has_side_effects=True, vmem_limit_bytes=VMEM_BYTES
        ),
        name="masked_cross",
    )(support.T, obs_factor, ctrl_factor)
    return jnp.swapaxes(turned, 1, 2)


def mask_local(obs_factor, ctrl_factor, support):
    local_cols = ctrl_factor.shape[1]
    total_cols = lax.axis_size("snap") * local_cols
    col_block = total_cols // support.shape[1]
    blocks_here = local_cols // col_block
    first_block = lax.axis_index("snap") * blocks_here
    owned_blocks = lax.dynamic_slice_in_dim(support, first_block, blocks_here, 1)
    keep_mask = jnp.repeat(owned_blocks, col_block, axis=1).astype(jnp.bfloat16)
    row_blocks = support.shape[0]
    total_rows, windows, _ = obs_factor.shape
    obs_kept = (
        obs_factor.reshape(row_blocks, total_rows // row_blocks, windows, local_cols)
        * keep_mask[:, None, None, :]
    )
    ctrl_kept = (
        ctrl_factor.reshape(row_blocks, total_rows // row_blocks, local_cols)
        * keep_mask[:, None, :]
    )
    return (obs_kept.reshape(obs_factor.shape), ctrl_kept.reshape(ctrl_factor.shape))


def general_local(obs_factor, ctrl_factor, support):
    obs_kept, ctrl_kept = mask_local(obs_factor, ctrl_factor, support)
    band_rows = jnp.einsum(
        "rwi,rj->wij",
        obs_kept,
        lax.all_gather(ctrl_kept, "snap", axis=1, tiled=True),
        preferred_element_type=jnp.float32,
    )
    return lax.psum_scatter(band_rows, "state", scatter_dimension=2, tiled=True)


def solution(mesh):
    in_specs = (P("state", None, "snap"), P("state", "snap"), P("state", None))
    out_specs = P(None, "snap", "state")
    fits = mesh.shape["state"] == PLANE and mesh.shape["snap"] == LINE
    body = plane_local if fits else general_local
    return jax.shard_map(body, mesh=mesh, in_specs=in_specs, out_specs=out_specs, check_vma=False)
```

profile of v0, /device:TPU:24, one launch (start us, length us, event | category | flops | bytes accessed | tf_op | source)
XLA Modules:
  0.0 32.4 jit_solution(5900077982733927851)
XLA Ops:
  0.0 0.0 copy-start
  0.0 0.9 %copy-done = bf16[1024,128]{1,0:T(8,128)(2,1)S(1)} copy-done((bf16[1024,128]{1,0:T(8,128)(2,1)S(1)}, bf16[1024,128]{1,0:T(8,128)(2,1)}, u32[]{:S(2)}) %copy-start) | copy-done | bytes 262168
  1.0 0.0 copy-start.1
  1.0 0.7 %copy-done.1 = s32[8,4]{0,1:T(4,128)S(1)} copy-done((s32[8,4]{0,1:T(4,128)S(1)}, s32[8,4]{0,1:T(4,128)}, u32[]{:S(2)}) %copy-start.1) | copy-done | bytes 152
  1.6 30.1 %masked_cross.1 = f32[8,64,128]{2,1,0:T(8,128)S(1)} custom-call(s32[4,8]{1,0:T(4,128)S(1)} %bitcast.3, bf16[1024,8,128]{2,1,0:T(8,128)(2,1)} %obs_hbm.1, bf16[1024,128]{1,0:T(8,128)(2,1)S(1)} %copy-done), custom_call_target="tpu_custom_call" | custom-call | tf_op jit(solution)/shard_map/masked_cross/pallas_call | solution.py:374
  31.7 0.7 %copy.5 = f32[8,128,64]{1,2,0:T(8,128)} copy(f32[8,128,64]{1,2,0:T(8,128)S(1)} %bitcast.2) | data formatting | bytes 524288
Async XLA Ops:
  0.0 0.9 %copy-start = (bf16[1024,128]{1,0:T(8,128)(2,1)S(1)}, bf16[1024,128]{1,0:T(8,128)(2,1)}, u32[]{:S(2)}) copy-start(bf16[1024,128]{1,0:T(8,128)(2,1)} %ctrl_hbm.1) | copy-start | bytes 786436
  1.0 0.7 %copy-start.1 = (s32[8,4]{0,1:T(4,128)S(1)}, s32[8,4]{0,1:T(4,128)}, u32[]{:S(2)}) copy-start(s32[8,4]{0,1:T(4,128)} %param.5) | copy-start | bytes 388
where the time goes:
time: 32.6 us; the launch traced here: 32.4 us
  Pallas kernels  30.1 us (92%)
  local copies, waits for them, and re-layouts  2.34 us (7%)
    pallas_call x1, Pallas kernels, plane_local(): pl.pallas_call(cross_kernel, out_shape=jax.ShapeDtypeStruct((windows, col...  30.1 us
    unnamed x5, local copies, waits for them, and re-layouts  2.34 us

commit v1 on v0

--- a/solution.py
+++ b/solution.py
@@ -17,15 +17,16 @@
 BEHIND_MIDDLE = 4
 BEHIND_END = 2
 PAIR = 2
-RELAY_AT = {2: 0, 3: 2, 4: 8, 5: 8, 6: 10, 7: 12}
-VMEM_BYTES = 52 * 1024 * 1024
+RELAY_AT = {2: 4, 3: 6, 4: 10, 5: 12, 6: 13, 7: 14}
+VMEM_BYTES = 54900 * 1024
 
 
 def cross_kernel(
-    support,
+    support_hbm,
     obs_hbm,
     ctrl_hbm,
     out,
+    support,
     obs_raw,
     ctrl_raw,
     wide,
@@ -49,7 +50,7 @@
 ):
     s = lax.axis_index("state")
     z = lax.axis_index("snap")
-    row_blocks = support.shape[1]
+    row_blocks = support_hbm.shape[1]
     rows, windows, cols = obs_hbm.shape
     block = rows // row_blocks
     piece = ctrl_t.shape[3]
@@ -70,10 +71,11 @@
         span = pl.ds(k * block, block)
         return pltpu.make_async_copy(obs_hbm.at[span], obs_raw.at[span], ld_sem.at[k])
 
+    def load_support():
+        return pltpu.make_async_copy(support_hbm, support, ld_sem.at[row_blocks + 1])
+
     load_ctrl().start()
-    for k in range(row_blocks):
-        load_obs(k).start()
-
+    load_support().start()
     barrier = pltpu.get_barrier_semaphore()
 
     def greet(state, snap):
@@ -93,6 +95,10 @@
         greet(s, z + 1)
         greet(pair, z + 1)
 
+    for k in range(row_blocks):
+        load_obs(k).start()
+
+    load_support().wait()
     load_ctrl().wait()
     for k in range(row_blocks):
         span = slice(k * block, (k + 1) * block)
@@ -235,7 +241,7 @@
 
     def finished(t):
         behind = jnp.where(middle, BEHIND_MIDDLE, BEHIND_END)
-        return jnp.maximum(jnp.minimum(2 * t - 3 * QS, t - behind), 0)
+        return jnp.maximum(jnp.minimum(2 * t - 3 * QS, t - behind + 1), 0)
 
     def finish(t, _):
         b = block_at(t // QS)
@@ -253,26 +259,26 @@
     tile = 2 * cols
     width = obs.shape[2]
 
-    def turn(t, before, count):
+    def turn(t, before, after, count):
         b = block_at(t // QS)
         q = t % QS
 
-        for k, when in RELAY_AT.items():
-
-            @pl.when(t == when)
-            def _():
-                pass_on(1 + k // QS, k % QS)
-
-        @pl.when(t < QS)
-        def _():
+        if count == QS:
             for i in range(count):
                 arrived(b, q + i, 1 - h)
-
-        @pl.when(jnp.logical_and(t >= QS, jnp.logical_not(middle)))
-        def _():
-            for i in range(count):
+        else:
+            for k, when in RELAY_AT.items():
+
+                @pl.when(t == when)
+                def _():
+                    pass_on(1 + k // QS, k % QS)
+
+        if count == 1:
+
+            @pl.when(jnp.logical_not(middle))
+            def _():
                 for hs in range(CORES):
-                    arrived(b, q + i, hs)
+                    arrived(b, q, hs)
 
         left = [
             ctrl_t[b, pl.ds(q, count), hs].reshape(count * piece, obs.shape[1])
@@ -303,25 +309,26 @@
                 half_copy(0, q + i, 0, b, y_next).start()
                 half_copy(1, q + i, 1, b, x_next).start()
 
-        lax.fori_loop(before, finished(t), finish, 0)
+        if count < QS:
+            lax.fori_loop(before, after, finish, 0)
         return 0
 
-    paired = (LINE - 1) * QS
+    singles = jnp.where(middle, (LINE - 1) * QS, QS)
 
     def double(i, _):
-        t = i * PAIR
-        return turn(t, finished(t - PAIR), PAIR)
-
-    def single(i, _):
-        t = paired + i
-        return turn(t, finished(jnp.where(i == 0, t - PAIR, t - 1)), 1)
+        t = QS + i * PAIR
+        return turn(t, finished(t - 1), finished(t + PAIR - 1), PAIR)
+
+    def single(t, _):
+        return turn(t, finished(t - 1), finished(t), 1)
 
     for k in range(RELAY_FROM):
         pass_on(1, k)
     for k in range(row_blocks):
         obs_copy(k).wait_recv()
-    lax.fori_loop(0, paired // PAIR, double, 0)
-    lax.fori_loop(0, QS, single, 0)
+    turn(0, 0, 0, QS)
+    lax.fori_loop(0, (singles - QS) // PAIR, double, 0)
+    lax.fori_loop(singles, LINE * QS, single, 0)
     lax.fori_loop(finished(LINE * QS - 1), LINE * QS, finish, 0)
 
     for q in range(QS):
@@ -375,12 +382,13 @@
         cross_kernel,
         out_shape=jax.ShapeDtypeStruct((windows, cols // CORES, cols), f32),
         in_specs=[
-            pl.BlockSpec(memory_space=pltpu.SMEM),
+            pl.BlockSpec(memory_space=pltpu.HBM),
             pl.BlockSpec(memory_space=pltpu.HBM),
             pl.BlockSpec(memory_space=pltpu.HBM),
         ],
         out_specs=pl.BlockSpec(memory_space=pltpu.VMEM),
         scratch_shapes=[
+            pltpu.SMEM((support.shape[1], row_blocks), jnp.int32),
             pltpu.VMEM((rows, windows, cols), bf16),
             pltpu.VMEM((rows, cols), bf16),
             pltpu.VMEM((rows // row_blocks * windows, cols), f32),
@@ -390,7 +398,7 @@
             pltpu.VMEM((LINE, QS, 2, piece // 2, width), f32),
             pltpu.VMEM((2, QS, piece // 2, width), f32),
             pltpu.VMEM((2, QS, 2, piece // 2, width), f32),
-            dma((row_blocks + 1,)),
+            dma((row_blocks + 2,)),
             dma((row_blocks,)),
             dma((row_blocks,)),
             dma((2, QS, CORES)),

time: 32.6 us -> 30.4 us (0.933)
  Pallas kernels: 30.1 us -> 28.8 us
  local copies, waits for them, and re-layouts: 2.34 us -> 1.39 us
    pallas_call x1, Pallas kernels: 30.1 us -> 28.8 us  [plane_local(): pl.pallas_call(cross_kernel, out_shape=jax.ShapeDtypeStruct((windows, col...]
    unnamed x5 -> x3, local copies, waits for them, and re-layouts: 2.34 us -> 1.39 us
where the time goes in v1:
time: 30.4 us; the launch traced here: 30.2 us
  Pallas kernels  28.8 us (95%)
  local copies, waits for them, and re-layouts  1.39 us (5%)
    pallas_call x1, Pallas kernels, plane_local(): pl.pallas_call(cross_kernel, out_shape=jax.ShapeDtypeStruct((windows, col...  28.8 us
    unnamed x3, local copies, waits for them, and re-layouts  1.39 us

profile of v1, /device:TPU:24, one launch (start us, length us, event | category | flops | bytes accessed | tf_op | source)
XLA Modules:
  0.0 30.2 jit_solution(17591506909019252908)
XLA Ops:
  0.0 0.0 copy-start
  0.0 0.7 %copy-done = s32[8,4]{0,1:T(4,128)S(1)} copy-done((s32[8,4]{0,1:T(4,128)S(1)}, s32[8,4]{0,1:T(4,128)}, u32[]{:S(2)}) %copy-start) | copy-done | bytes 152
  0.7 28.8 %masked_cross.1 = f32[8,64,128]{2,1,0:T(8,128)S(1)} custom-call(s32[4,8]{1,0:T(4,128)S(1)} %bitcast.3, bf16[1024,8,128]{2,1,0:T(8,128)(2,1)} %obs_hbm.1, bf16[1024,128]{1,0:T(8,128)(2,1)} %ctrl_hbm.1), custom_call_target="tpu_custom_call" | custom-call | tf_op jit(solution)/shard_map/masked_cross/pallas_call | solution.py:381
  29.5 0.7 %copy.5 = f32[8,128,64]{1,2,0:T(8,128)} copy(f32[8,128,64]{1,2,0:T(8,128)S(1)} %bitcast.2) | data formatting | bytes 524288
Async XLA Ops:
  0.0 0.7 %copy-start = (s32[8,4]{0,1:T(4,128)S(1)}, s32[8,4]{0,1:T(4,128)}, u32[]{:S(2)}) copy-start(s32[8,4]{0,1:T(4,128)} %param.5) | copy-start | bytes 388

commit v2 on v1

--- a/solution.py
+++ b/solution.py
@@ -13,11 +13,14 @@
 PLANE = CORES * SIDE * SIDE
 LINE = SIDE * SIDE
 QS = 4
-RELAY_FROM = QS // 2
-BEHIND_MIDDLE = 4
-BEHIND_END = 2
+LAG_MIDDLE = 3
+RAMP_MIDDLE = 12
+LAG_END = 1
+RAMP_END = 12
 PAIR = 2
-RELAY_AT = {2: 4, 3: 6, 4: 10, 5: 12, 6: 13, 7: 14}
+RELAY_AT = ((1, 2, 4), (1, 3, 6), (2, 0, 10), (2, 1, 12), (2, 2, 13), (2, 3, 14))
+EARLY = QS // 2
+SINGLES_MIDDLE = (LINE - 1) * QS
 VMEM_BYTES = 54900 * 1024
 
 
@@ -121,8 +124,8 @@
         return pltpu.make_async_remote_copy(
             src_ref=own_t.at[g * QS + q],
             dst_ref=ctrl_t.at[z, q, h],
-            send_sem=own_send.at[side, q, g],
-            recv_sem=ctrl_recv.at[z, q, h],
+            send_sem=own_send.at[side],
+            recv_sem=ctrl_recv.at[z, q],
             device_id=(state, snap),
             device_id_type=MESH,
         )
@@ -131,8 +134,8 @@
         return pltpu.make_async_remote_copy(
             src_ref=own_t.at[(1 - h) * QS + q],
             dst_ref=ctrl_t.at[z, q, h],
-            send_sem=pair_send.at[q],
-            recv_sem=ctrl_recv.at[z, q, h],
+            send_sem=pair_send,
+            recv_sem=ctrl_recv.at[z, q],
             device_id=(pair, z),
             device_id_type=MESH,
         )
@@ -141,16 +144,26 @@
         return pltpu.make_async_remote_copy(
             src_ref=ctrl_t.at[b, q, hs],
             dst_ref=ctrl_t.at[b, q, hs],
-            send_sem=fwd_send.at[b, q, hs],
-            recv_sem=ctrl_recv.at[b, q, hs],
+            send_sem=fwd_send.at[b],
+            recv_sem=ctrl_recv.at[b, q],
             device_id=(s, snap),
             device_id_type=MESH,
         )
 
-    def arrived(b, q, hs):
-        fwd_copy(b, q, hs, z).wait_recv()
-
-    for q in range(QS):
+    def span_of(ref, send, recv):
+        return pltpu.make_async_remote_copy(
+            src_ref=ref,
+            dst_ref=ref,
+            send_sem=send,
+            recv_sem=recv,
+            device_id=(pair, z),
+            device_id_type=MESH,
+        )
+
+    def arrived(b, q):
+        span_of(ctrl_t.at[b, q], pair_send, ctrl_recv.at[b, q]).wait_recv()
+
+    def own_out(q):
         for g in range(CORES):
 
             @pl.when(z > 0)
@@ -162,6 +175,9 @@
                 own_copy(1, q, g).start()
 
     for q in range(QS):
+        own_out(q)
+
+    for q in range(QS):
         pair_copy(q).start()
         ctrl_t[z, q, h] = own_t[h * QS + q]
 
@@ -170,8 +186,8 @@
         return pltpu.make_async_remote_copy(
             src_ref=obs.at[h, span],
             dst_ref=obs.at[h, span],
-            send_sem=obs_send.at[k],
-            recv_sem=obs_recv.at[k],
+            send_sem=obs_send,
+            recv_sem=obs_recv,
             device_id=(pair, z),
             device_id_type=MESH,
         )
@@ -194,14 +210,14 @@
     def pass_on(d, q):
         @pl.when(jnp.logical_and(middle, z - d >= 0))
         def _():
+            arrived(z - d, q)
             for hs in range(CORES):
-                arrived(z - d, q, hs)
                 fwd_copy(z - d, q, hs, z + 1).start()
 
         @pl.when(jnp.logical_and(middle, z + d <= last))
         def _():
+            arrived(z + d, q)
             for hs in range(CORES):
-                arrived(z + d, q, hs)
                 fwd_copy(z + d, q, hs, z - 1).start()
 
     def block_at(k):
@@ -211,11 +227,14 @@
             z == 0, up, jnp.where(z == last, last - up, jnp.where(z == 1, one, last - one))
         )
 
+    def piece_at(t):
+        return block_at(t // QS), t % QS
+
     def half_copy(kind, q, rows_half, b, state):
         return pltpu.make_async_remote_copy(
             src_ref=part.at[b, q, rows_half],
             dst_ref=far.at[kind, q],
-            send_sem=half_send.at[kind, q],
+            send_sem=half_send,
             recv_sem=half_recv.at[kind, q],
             device_id=(state, z),
             device_id_type=MESH,
@@ -224,9 +243,9 @@
     def near_copy(kind, q, rows_half, b, state):
         return pltpu.make_async_remote_copy(
             src_ref=part.at[b, q, rows_half],
-            dst_ref=near.at[kind, q, rows_half],
-            send_sem=far_send.at[kind, q, rows_half],
-            recv_sem=far_recv.at[kind, q, rows_half],
+            dst_ref=near.at[q, kind, rows_half],
+            send_sem=far_send,
+            recv_sem=far_recv.at[q],
             device_id=(state, z),
             device_id_type=MESH,
         )
@@ -240,12 +259,12 @@
         return kind, beside, corner
 
     def finished(t):
-        behind = jnp.where(middle, BEHIND_MIDDLE, BEHIND_END)
-        return jnp.maximum(jnp.minimum(2 * t - 3 * QS, t - behind + 1), 0)
+        lag = jnp.where(middle, LAG_MIDDLE, LAG_END)
+        ramp = jnp.where(middle, RAMP_MIDDLE, RAMP_END)
+        return jnp.maximum(jnp.minimum(2 * t - ramp, t - lag), 0)
 
     def finish(t, _):
-        b = block_at(t // QS)
-        q = t % QS
+        b, q = piece_at(t)
         kind, beside, _ = role(b)
 
         @pl.when(beside)
@@ -260,25 +279,26 @@
     width = obs.shape[2]
 
     def turn(t, before, after, count):
-        b = block_at(t // QS)
-        q = t % QS
+        b, q = piece_at(t)
 
         if count == QS:
             for i in range(count):
-                arrived(b, q + i, 1 - h)
-        else:
-            for k, when in RELAY_AT.items():
+                span_of(
+                    ctrl_t.at[b, i, 1 - h], pair_send, ctrl_recv.at[b, i]
+                ).wait_recv()
+
+        if count < QS:
+            for d, k, when in RELAY_AT:
 
                 @pl.when(t == when)
                 def _():
-                    pass_on(1 + k // QS, k % QS)
+                    pass_on(d, k)
 
         if count == 1:
 
             @pl.when(jnp.logical_not(middle))
             def _():
-                for hs in range(CORES):
-                    arrived(b, q, hs)
+                arrived(b, q)
 
         left = [
             ctrl_t[b, pl.ds(q, count), hs].reshape(count * piece, obs.shape[1])
@@ -313,7 +333,7 @@
             lax.fori_loop(before, after, finish, 0)
         return 0
 
-    singles = jnp.where(middle, (LINE - 1) * QS, QS)
+    singles = jnp.where(middle, SINGLES_MIDDLE, QS)
 
     def double(i, _):
         t = QS + i * PAIR
@@ -322,53 +342,45 @@
     def single(t, _):
         return turn(t, finished(t - 1), finished(t), 1)
 
-    for k in range(RELAY_FROM):
+    for k in range(EARLY):
         pass_on(1, k)
-    for k in range(row_blocks):
-        obs_copy(k).wait_recv()
+
+    span_of(obs.at[1 - h], obs_send, obs_recv).wait_recv()
     turn(0, 0, 0, QS)
     lax.fori_loop(0, (singles - QS) // PAIR, double, 0)
     lax.fori_loop(singles, LINE * QS, single, 0)
     lax.fori_loop(finished(LINE * QS - 1), LINE * QS, finish, 0)
 
     for q in range(QS):
+        span_of(near.at[q], far_send, far_recv.at[q]).wait_recv()
         for r in range(2):
-            for kind in range(2):
-                near_copy(kind, q, r, chip, s).wait_recv()
-            total = part[chip, q, r] + near[0, q, r] + near[1, q, r]
+            total = part[chip, q, r] + near[q, 0, r] + near[q, 1, r]
             base = (q * 2 + r) * (piece // 2)
             for w in range(windows):
                 out[w, base : base + piece // 2, :] = total[:, w * cols : (w + 1) * cols]
 
-    for q in range(QS):
-        for kind in range(2):
-            half_copy(kind, q, kind, chip, y_next).wait_send()
-            for r in range(2):
-                near_copy(kind, q, r, chip, y_next).wait_send()
-        pair_copy(q).wait_send()
-        for g in range(CORES):
-
-            @pl.when(z > 0)
-            def _():
-                own_copy(0, q, g).wait_send()
-
-            @pl.when(z < last)
-            def _():
-                own_copy(1, q, g).wait_send()
-
-        for d in range(1, LINE - 1):
-            for hs in range(CORES):
-
-                @pl.when(jnp.logical_and(middle, z - d >= 0))
-                def _():
-                    fwd_copy(z - d, q, hs, z).wait_send()
-
-                @pl.when(jnp.logical_and(middle, z + d <= last))
-                def _():
-                    fwd_copy(z + d, q, hs, z).wait_send()
-
-    for k in range(row_blocks):
-        obs_copy(k).wait_send()
+    span_of(part.at[0], half_send, half_send).wait_send()
+    span_of(near, far_send, far_send).wait_send()
+    span_of(own_t.at[pl.ds(0, QS)], pair_send, pair_send).wait_send()
+    span_of(obs.at[h], obs_send, obs_send).wait_send()
+
+    @pl.when(z > 0)
+    def _():
+        span_of(own_t, own_send.at[0], own_send.at[0]).wait_send()
+
+    @pl.when(z < last)
+    def _():
+        span_of(own_t, own_send.at[1], own_send.at[1]).wait_send()
+
+    for d in range(1, LINE - 1):
+
+        @pl.when(jnp.logical_and(middle, z - d >= 0))
+        def _():
+            span_of(ctrl_t.at[z - d], fwd_send.at[z - d], pair_send).wait_send()
+
+        @pl.when(jnp.logical_and(middle, z + d <= last))
+        def _():
+            span_of(ctrl_t.at[z + d], fwd_send.at[z + d], pair_send).wait_send()
 
 
 def plane_local(obs_factor, ctrl_factor, support):
@@ -397,18 +409,18 @@
             pltpu.VMEM((LINE, QS, CORES, piece, rows), bf16),
             pltpu.VMEM((LINE, QS, 2, piece // 2, width), f32),
             pltpu.VMEM((2, QS, piece // 2, width), f32),
-            pltpu.VMEM((2, QS, 2, piece // 2, width), f32),
+            pltpu.VMEM((QS, 2, 2, piece // 2, width), f32),
             dma((row_blocks + 2,)),
-            dma((row_blocks,)),
-            dma((row_blocks,)),
-            dma((2, QS, CORES)),
+            dma,
+            dma,
+            dma((2,)),
+            dma,
+            dma((LINE,)),
+            dma((LINE, QS)),
+            dma,
+            dma((2, QS)),
+            dma,
             dma((QS,)),
-            dma((LINE, QS, CORES)),
-            dma((LINE, QS, CORES)),
-            dma((2, QS)),
-            dma((2, QS)),
-            dma((2, QS, 2)),
-            dma((2, QS, 2)),
         ],
         compiler_params=pltpu.CompilerParams(
             collective_id=0, has_side_effects=True, vmem_limit_bytes=VMEM_BYTES

time: 30.4 us -> 29.3 us (0.964)
  Pallas kernels: 28.8 us -> 27.8 us
    pallas_call x1, Pallas kernels: 28.8 us -> 27.8 us  [plane_local(): pl.pallas_call(cross_kernel, out_shape=jax.ShapeDtypeStruct((windows, col...]
where the time goes in v2:
time: 29.3 us; the launch traced here: 29.2 us
  Pallas kernels  27.8 us (95%)
  local copies, waits for them, and re-layouts  1.39 us (5%)
    pallas_call x1, Pallas kernels, plane_local(): pl.pallas_call(cross_kernel, out_shape=jax.ShapeDtypeStruct((windows, col...  27.8 us
    unnamed x3, local copies, waits for them, and re-layouts  1.39 us

profile of v2, /device:TPU:24, one launch (start us, length us, event | category | flops | bytes accessed | tf_op | source)
XLA Modules:
  0.0 29.2 jit_solution(17324573150044574281)
XLA Ops:
  0.0 0.0 copy-start
  0.0 0.7 %copy-done = s32[8,4]{0,1:T(4,128)S(1)} copy-done((s32[8,4]{0,1:T(4,128)S(1)}, s32[8,4]{0,1:T(4,128)}, u32[]{:S(2)}) %copy-start) | copy-done | bytes 152
  0.7 27.8 %masked_cross.1 = f32[8,64,128]{2,1,0:T(8,128)S(1)} custom-call(s32[4,8]{1,0:T(4,128)S(1)} %bitcast.3, bf16[1024,8,128]{2,1,0:T(8,128)(2,1)} %obs_hbm.1, bf16[1024,128]{1,0:T(8,128)(2,1)} %ctrl_hbm.1), custom_call_target="tpu_custom_call" | custom-call | tf_op jit(solution)/shard_map/masked_cross/pallas_call | solution.py:393
  28.4 0.7 %copy.5 = f32[8,128,64]{1,2,0:T(8,128)} copy(f32[8,128,64]{1,2,0:T(8,128)S(1)} %bitcast.2) | data formatting | bytes 524288
Async XLA Ops:
  0.0 0.7 %copy-start = (s32[8,4]{0,1:T(4,128)S(1)}, s32[8,4]{0,1:T(4,128)}, u32[]{:S(2)}) copy-start(s32[8,4]{0,1:T(4,128)} %param.5) | copy-start | bytes 388
